TPU v7x, 32 devices: a whole 2x2x4 slice. The times are simulated.
32 devices in a mesh: lev: 8 (over z, x), tile: 4 (over y, core).
Axes of the slice: x: 2, y: 2, z: 4, core: 2. Of those that a mesh axis runs over, the one named last changes fastest.
Arguments:
- increment: float32 [144, 96, 1440], P('lev', 'tile'), may hold values from -6 to 6
- kappa: float32 [144], P('lev'), may hold values from 0.02 to 0.24
- balance: float32 [144, 144], replicated, may hold values from -0.5 to 0.5
- correlation: float32 [144, 144], replicated, may hold values from -0.5 to 0.5
- ground_level: int32 [96, 1440], P('tile'), may hold values from 72 to 144
Outputs:
- covaried: float32 [144, 96, 1440], P('lev', 'tile')
Inputs may be any that keep to these rules, and one draw needn't show every extreme that they name: Levels from ground_level of a column down to the last one lie below ground.
All inputs are finite; a program needn't handle non-finite values.
Results may differ from a plain program's by a relative error of at most 0.00019.
Values sent between devices are 32-bit elements; how exact they have to be, the bound alone decides.
No kernel may reach another device: no remote copies, remote signals or barrier semaphores. Data moves between devices by JAX's collectives and lax.ppermute only.
A program may use at most 64 MiB of HBM per device.

v0:
```python
import jax
import jax.numpy as jnp
from jax import lax
from jax.sharding import PartitionSpec as P

PASSES = 10


def padded_2(value, sides, width):
    for axis, dim in sides:
        size, length = (lax.axis_size(axis), value.shape[dim])
        up = [(i, (i + 1) % size) for i in range(size - 1)]
        down = [(j, i) for i, j in up]
        last = lax.slice_in_dim(value, length - width, length, axis=dim)
        leading = lax.slice_in_dim(value, 0, width, axis=dim)
        before = lax.ppermute(last, axis, up)
        after = lax.ppermute(leading, axis, down)
        value = jnp.concatenate([before, value, after], axis=dim)
    return value


def local(increment, kappa, balance, correlation, ground_level):
    levels_here, lat_rows, lon_cells = increment.shape
    diffusivity = kappa[:, None, None]
    tile_start = lax.axis_index("tile") * lat_rows
    lat_total = lat_rows * lax.axis_size("tile")

    def sweep(padded, first_row):
        middle_rows = padded[:, 1:-1]
        beside = (
            padded[:, 2:]
            + padded[:, :-2]
            + jnp.roll(middle_rows, 1, 2)
            + jnp.roll(middle_rows, -1, 2)
        )
        result = middle_rows + diffusivity * (beside - 4.0 * middle_rows)
        global_rows = first_row + 1 + lax.broadcasted_iota(jnp.int32, (1, result.shape[1], 1), 1)
        inside = (global_rows >= 0) & (global_rows < lat_total)
        return jnp.where(inside, result, jnp.zeros((), jnp.float32))

    def two_passes(counter, state_field):
        padded = padded_2(state_field, (("tile", 1),), 2)
        return sweep(sweep(padded, tile_start - 2), tile_start - 1)

    smoothed = lax.fori_loop(0, PASSES // 2, two_passes, increment)
    flattened = smoothed.reshape(levels_here, lat_rows * lon_cells)
    group_size = lax.axis_size("lev")
    block_cols = lat_rows * lon_cells // group_size
    col_start = lax.axis_index("lev") * block_cols
    ground = lax.dynamic_slice_in_dim(
        ground_level.reshape(lat_rows * lon_cells), col_start, block_cols
    )
    total_levels = balance.shape[0]
    columns = lax.all_to_all(flattened, "lev", split_axis=1, concat_axis=0, tiled=True)
    mixed_cols = jnp.dot(
        balance, columns, precision=lax.Precision.HIGHEST, preferred_element_type=jnp.float32
    )
    mixed_cols = jnp.dot(
        correlation, mixed_cols, precision=lax.Precision.HIGHEST, preferred_element_type=jnp.float32
    )
    level_index = lax.broadcasted_iota(jnp.int32, (total_levels, 1), 0)
    mixed_cols = jnp.where(level_index < ground[None, :], mixed_cols, jnp.zeros((), jnp.float32))
    restored = lax.all_to_all(mixed_cols, "lev", split_axis=0, concat_axis=1, tiled=True)
    return restored.reshape(levels_here, lat_rows, lon_cells)


def solution(mesh):
    return jax.shard_map(
        local,
        mesh=mesh,
        in_specs=(P("lev", "tile", None), P("lev"), P(), P(), P("tile", None)),
        out_specs=P("lev", "tile", None),
        check_vma=False,
    )
```

profile of v0, /device:TPU:0, one launch (start us, length us, event | category | flops | bytes accessed | tf_op | source)
XLA Modules:
  0.0 272.3 jit_solution(930868567146244389)
XLA Ops:
  1.8 89.0 %while.12 = (s32[]{:T(128)}, f32[18,24,1440]{2,1,0:T(8,128)S(1)}, s32[]{:T(128)}, s32[]{:T(128)}, f32[18,1,1]{0,2,1:T(1,128)S(1)}, /*index=5*/s32[]{:T(128)}) while((s32[]{:T(128)}, f32[18,24,1440]{2,1,0:T(8,128)S(1)}, s32[]{:T(128)}, s32[]{:T(128)}, f32[18,1,1]{0,2,1:T(1,128)S(1)}, /*index=5*/s32[]{:T(128)}) %tuple.41), condition=%wide.region_1.2_spmd, body=%wide.region_0.1_spmd.sunk | while | flops 18455240 | bytes 57635248 | solution.py:45
  3.9 3.0 %collective-permute-start.1 = (f32[18,2,1440]{2,1,0:T(2,128)S(1)}, f32[18,2,1440]{2,1,0:T(2,128)S(1)}, u32[]{:S(2)}, u32[]{:S(2)}) collective-permute-start(f32[18,2,1440]{2,1,0:T(2,128)S(1)} %get-tuple-element.123), channel_id=1, source_target_pairs={{0,1},{1,2},{2,3},{4,5},{5,6},{6,7},{8,9},{9,10},{10,11},{12,13},{... | collective-permute-start | bytes 622088 | tf_op jit(solution)/shard_map/while/body/eval_jaxpr/ppermute | solution.py:16
  8.6 1.8 fusion.31
  10.4 3.1 %fusion.32 = f32[18,26,1440]{2,1,0:T(8,128)S(1)} fusion(f32[18,2,1440]{2,1,0:T(2,128)S(1)} %collective-permute-done, f32[18,24,1440]{2,1,0:T(8,128)S(1)} %get-tuple-element.137, f32[18,2,1440]{2,1,0:T(2,128)S(1)} %collective-permute-done.1, f32[18,26,1439]{2,1,0:T(8,128)S(1)} %get-tuple-element.124, f32[18,26,1439]{2,1,0:T(8,128)S(1)} %get-tuple-element.125, ...), kind=kLoop, calls=%fused_computation.6.clone.1 | loop fusion | flops 10782720 | bytes 13682114 | tf_op jit(solution)/shard_map/while/body/eval_jaxpr/jit(_where)/select_n | solution.py:39
  18.7 6.9 %collective-permute-start.1 = (f32[18,2,1440]{2,1,0:T(2,128)S(1)}, f32[18,2,1440]{2,1,0:T(2,128)S(1)}, u32[]{:S(2)}, u32[]{:S(2)}) collective-permute-start(f32[18,2,1440]{2,1,0:T(2,128)S(1)} %get-tuple-element.123), channel_id=1, source_target_pairs={{0,1},{1,2},{2,3},{4,5},{5,6},{6,7},{8,9},{9,10},{10,11},{12,13},{... | collective-permute-start | bytes 622088 | tf_op jit(solution)/shard_map/while/body/eval_jaxpr/ppermute | solution.py:16
  27.3 1.8 fusion.31
  29.1 3.1 %fusion.32 = f32[18,26,1440]{2,1,0:T(8,128)S(1)} fusion(f32[18,2,1440]{2,1,0:T(2,128)S(1)} %collective-permute-done, f32[18,24,1440]{2,1,0:T(8,128)S(1)} %get-tuple-element.137, f32[18,2,1440]{2,1,0:T(2,128)S(1)} %collective-permute-done.1, f32[18,26,1439]{2,1,0:T(8,128)S(1)} %get-tuple-element.124, f32[18,26,1439]{2,1,0:T(8,128)S(1)} %get-tuple-element.125, ...), kind=kLoop, calls=%fused_computation.6.clone.1 | loop fusion | flops 10782720 | bytes 13682114 | tf_op jit(solution)/shard_map/while/body/eval_jaxpr/jit(_where)/select_n | solution.py:39
  37.3 6.8 %collective-permute-start.1 = (f32[18,2,1440]{2,1,0:T(2,128)S(1)}, f32[18,2,1440]{2,1,0:T(2,128)S(1)}, u32[]{:S(2)}, u32[]{:S(2)}) collective-permute-start(f32[18,2,1440]{2,1,0:T(2,128)S(1)} %get-tuple-element.123), channel_id=1, source_target_pairs={{0,1},{1,2},{2,3},{4,5},{5,6},{6,7},{8,9},{9,10},{10,11},{12,13},{... | collective-permute-start | bytes 622088 | tf_op jit(solution)/shard_map/while/body/eval_jaxpr/ppermute | solution.py:16
  45.8 1.8 fusion.31
  47.6 3.1 %fusion.32 = f32[18,26,1440]{2,1,0:T(8,128)S(1)} fusion(f32[18,2,1440]{2,1,0:T(2,128)S(1)} %collective-permute-done, f32[18,24,1440]{2,1,0:T(8,128)S(1)} %get-tuple-element.137, f32[18,2,1440]{2,1,0:T(2,128)S(1)} %collective-permute-done.1, f32[18,26,1439]{2,1,0:T(8,128)S(1)} %get-tuple-element.124, f32[18,26,1439]{2,1,0:T(8,128)S(1)} %get-tuple-element.125, ...), kind=kLoop, calls=%fused_computation.6.clone.1 | loop fusion | flops 10782720 | bytes 13682114 | tf_op jit(solution)/shard_map/while/body/eval_jaxpr/jit(_where)/select_n | solution.py:39
  55.9 6.8 %collective-permute-start.1 = (f32[18,2,1440]{2,1,0:T(2,128)S(1)}, f32[18,2,1440]{2,1,0:T(2,128)S(1)}, u32[]{:S(2)}, u32[]{:S(2)}) collective-permute-start(f32[18,2,1440]{2,1,0:T(2,128)S(1)} %get-tuple-element.123), channel_id=1, source_target_pairs={{0,1},{1,2},{2,3},{4,5},{5,6},{6,7},{8,9},{9,10},{10,11},{12,13},{... | collective-permute-start | bytes 622088 | tf_op jit(solution)/shard_map/while/body/eval_jaxpr/ppermute | solution.py:16
  64.3 1.8 fusion.31
  66.1 3.1 %fusion.32 = f32[18,26,1440]{2,1,0:T(8,128)S(1)} fusion(f32[18,2,1440]{2,1,0:T(2,128)S(1)} %collective-permute-done, f32[18,24,1440]{2,1,0:T(8,128)S(1)} %get-tuple-element.137, f32[18,2,1440]{2,1,0:T(2,128)S(1)} %collective-permute-done.1, f32[18,26,1439]{2,1,0:T(8,128)S(1)} %get-tuple-element.124, f32[18,26,1439]{2,1,0:T(8,128)S(1)} %get-tuple-element.125, ...), kind=kLoop, calls=%fused_computation.6.clone.1 | loop fusion | flops 10782720 | bytes 13682114 | tf_op jit(solution)/shard_map/while/body/eval_jaxpr/jit(_where)/select_n | solution.py:39
  74.4 6.8 %collective-permute-start.1 = (f32[18,2,1440]{2,1,0:T(2,128)S(1)}, f32[18,2,1440]{2,1,0:T(2,128)S(1)}, u32[]{:S(2)}, u32[]{:S(2)}) collective-permute-start(f32[18,2,1440]{2,1,0:T(2,128)S(1)} %get-tuple-element.123), channel_id=1, source_target_pairs={{0,1},{1,2},{2,3},{4,5},{5,6},{6,7},{8,9},{9,10},{10,11},{12,13},{... | collective-permute-start | bytes 622088 | tf_op jit(solution)/shard_map/while/body/eval_jaxpr/ppermute | solution.py:16
  84.6 3.1 %fusion.32 = f32[18,26,1440]{2,1,0:T(8,128)S(1)} fusion(f32[18,2,1440]{2,1,0:T(2,128)S(1)} %collective-permute-done, f32[18,24,1440]{2,1,0:T(8,128)S(1)} %get-tuple-element.137, f32[18,2,1440]{2,1,0:T(2,128)S(1)} %collective-permute-done.1, f32[18,26,1439]{2,1,0:T(8,128)S(1)} %get-tuple-element.124, f32[18,26,1439]{2,1,0:T(8,128)S(1)} %get-tuple-element.125, ...), kind=kLoop, calls=%fused_computation.6.clone.1 | loop fusion | flops 10782720 | bytes 13682114 | tf_op jit(solution)/shard_map/while/body/eval_jaxpr/jit(_where)/select_n | solution.py:39
  90.8 1.9 all_to_all.26
  92.7 4.2 %copy.8 = f32[18,8,4320]{2,0,1:T(8,128)} copy(f32[18,8,4320]{2,1,0:T(8,128)} %all_to_all.26) | data formatting | bytes 4976640 | tf_op jit(solution)/shard_map/all_to_all | solution.py:54
  96.9 5.8 %all-to-all-start = ((f32[18,8,4320]{2,0,1:T(8,128)}), f32[18,8,4320]{2,0,1:T(8,128)S(1)}, u32[]{:S(2)}, u32[]{:S(2)}) async-start(f32[18,8,4320]{2,0,1:T(8,128)} %copy.8), calls=%async_computation | async-start | bytes 6684672 | tf_op jit(solution)/shard_map/all_to_all | solution.py:54
  105.2 71.3 %all-to-all-done = f32[18,8,4320]{2,0,1:T(8,128)S(1)} async-done(((f32[18,8,4320]{2,0,1:T(8,128)}), f32[18,8,4320]{2,0,1:T(8,128)S(1)}, u32[]{:S(2)}, u32[]{:S(2)}) %all-to-all-start) | async-done | bytes 2488352 | tf_op jit(solution)/shard_map/all_to_all | solution.py:54
  178.1 4.2 %fusion.19 = f32[4320,144]{0,1:T(8,128)S(1)} fusion(f32[144,4320]{1,0:T(8,128)} %all_to_all.29, f32[144,144]{1,0:T(8,128)S(1)} %copy-done), kind=kOutput, calls=%fused_computation.30 | convolution fusion | flops 1074954240 | bytes 5059584 | tf_op jit(solution)/shard_map/dot_general | solution.py:55
  182.3 3.9 %fusion.14 = f32[144,4320]{1,0:T(8,128)} fusion(f32[4320,144]{0,1:T(8,128)S(1)} %fusion.19, f32[144,144]{1,0:T(8,128)S(1)} %copy-done.2, s32[4320]{0:T(1024)S(1)} %dynamic_slice.3), kind=kOutput, calls=%fused_computation.24 | convolution fusion | flops 1076198400 | bytes 5076864 | tf_op jit(solution)/shard_map/dot_general | solution.py:58
  186.2 1.9 all_to_all.30
  188.1 81.2 %all_to_all.35 = f32[8,18,4320]{2,1,0:T(8,128)S(1)} all-to-all(f32[8,18,4320]{2,1,0:T(8,128)S(1)} %all_to_all.30), channel_id=1, replica_groups=mesh['lev'=8,'tile'=4] {'lev'}, dimensions={0} | all-to-all | bytes 4976640 | tf_op jit(solution)/shard_map/all_to_all | solution.py:63
  270.1 2.3 reshape.39
  (63 shorter events, 42.3 us)
Async XLA Ops:
  0.0 178.1 %copy-start = (f32[144,144]{1,0:T(8,128)S(1)}, f32[144,144]{1,0:T(8,128)}, u32[]{:S(2)}) copy-start(f32[144,144]{1,0:T(8,128)} %param.9) | copy-start | bytes 248836
  0.0 1.8 copy-start.1
  0.0 1.8 copy-start.3
  2.6 4.4 %collective-permute-start = (f32[18,2,1440]{2,1,0:T(2,128)}, f32[18,2,1440]{2,1,0:T(2,128)S(1)}, u32[]{:S(2)}, u32[]{:S(2)}) collective-permute-start(f32[18,2,1440]{2,1,0:T(2,128)} %get-tuple-element.122), channel_id=1, source_target_pairs={{1,0},{2,1},{3,2},{5,4},{6,5},{7,6},{9,8},{10,9},{11,10},{13,12},{... | collective-permute-start | bytes 622088 | tf_op jit(solution)/shard_map/while/body/eval_jaxpr/ppermute | solution.py:17
  3.9 4.1 %collective-permute-start.1 = (f32[18,2,1440]{2,1,0:T(2,128)S(1)}, f32[18,2,1440]{2,1,0:T(2,128)S(1)}, u32[]{:S(2)}, u32[]{:S(2)}) collective-permute-start(f32[18,2,1440]{2,1,0:T(2,128)S(1)} %get-tuple-element.123), channel_id=1, source_target_pairs={{0,1},{1,2},{2,3},{4,5},{5,6},{6,7},{8,9},{9,10},{10,11},{12,13},{... | collective-permute-start | bytes 622088 | tf_op jit(solution)/shard_map/while/body/eval_jaxpr/ppermute | solution.py:16
  17.4 8.3 %collective-permute-start = (f32[18,2,1440]{2,1,0:T(2,128)}, f32[18,2,1440]{2,1,0:T(2,128)S(1)}, u32[]{:S(2)}, u32[]{:S(2)}) collective-permute-start(f32[18,2,1440]{2,1,0:T(2,128)} %get-tuple-element.122), channel_id=1, source_target_pairs={{1,0},{2,1},{3,2},{5,4},{6,5},{7,6},{9,8},{10,9},{11,10},{13,12},{... | collective-permute-start | bytes 622088 | tf_op jit(solution)/shard_map/while/body/eval_jaxpr/ppermute | solution.py:17
  18.7 8.0 %collective-permute-start.1 = (f32[18,2,1440]{2,1,0:T(2,128)S(1)}, f32[18,2,1440]{2,1,0:T(2,128)S(1)}, u32[]{:S(2)}, u32[]{:S(2)}) collective-permute-start(f32[18,2,1440]{2,1,0:T(2,128)S(1)} %get-tuple-element.123), channel_id=1, source_target_pairs={{0,1},{1,2},{2,3},{4,5},{5,6},{6,7},{8,9},{9,10},{10,11},{12,13},{... | collective-permute-start | bytes 622088 | tf_op jit(solution)/shard_map/while/body/eval_jaxpr/ppermute | solution.py:16
  36.1 8.1 %collective-permute-start = (f32[18,2,1440]{2,1,0:T(2,128)}, f32[18,2,1440]{2,1,0:T(2,128)S(1)}, u32[]{:S(2)}, u32[]{:S(2)}) collective-permute-start(f32[18,2,1440]{2,1,0:T(2,128)} %get-tuple-element.122), channel_id=1, source_target_pairs={{1,0},{2,1},{3,2},{5,4},{6,5},{7,6},{9,8},{10,9},{11,10},{13,12},{... | collective-permute-start | bytes 622088 | tf_op jit(solution)/shard_map/while/body/eval_jaxpr/ppermute | solution.py:17
  37.3 7.9 %collective-permute-start.1 = (f32[18,2,1440]{2,1,0:T(2,128)S(1)}, f32[18,2,1440]{2,1,0:T(2,128)S(1)}, u32[]{:S(2)}, u32[]{:S(2)}) collective-permute-start(f32[18,2,1440]{2,1,0:T(2,128)S(1)} %get-tuple-element.123), channel_id=1, source_target_pairs={{0,1},{1,2},{2,3},{4,5},{5,6},{6,7},{8,9},{9,10},{10,11},{12,13},{... | collective-permute-start | bytes 622088 | tf_op jit(solution)/shard_map/while/body/eval_jaxpr/ppermute | solution.py:16
  54.6 8.1 %collective-permute-start = (f32[18,2,1440]{2,1,0:T(2,128)}, f32[18,2,1440]{2,1,0:T(2,128)S(1)}, u32[]{:S(2)}, u32[]{:S(2)}) collective-permute-start(f32[18,2,1440]{2,1,0:T(2,128)} %get-tuple-element.122), channel_id=1, source_target_pairs={{1,0},{2,1},{3,2},{5,4},{6,5},{7,6},{9,8},{10,9},{11,10},{13,12},{... | collective-permute-start | bytes 622088 | tf_op jit(solution)/shard_map/while/body/eval_jaxpr/ppermute | solution.py:17
  55.9 7.9 %collective-permute-start.1 = (f32[18,2,1440]{2,1,0:T(2,128)S(1)}, f32[18,2,1440]{2,1,0:T(2,128)S(1)}, u32[]{:S(2)}, u32[]{:S(2)}) collective-permute-start(f32[18,2,1440]{2,1,0:T(2,128)S(1)} %get-tuple-element.123), channel_id=1, source_target_pairs={{0,1},{1,2},{2,3},{4,5},{5,6},{6,7},{8,9},{9,10},{10,11},{12,13},{... | collective-permute-start | bytes 622088 | tf_op jit(solution)/shard_map/while/body/eval_jaxpr/ppermute | solution.py:16
  73.1 8.1 %collective-permute-start = (f32[18,2,1440]{2,1,0:T(2,128)}, f32[18,2,1440]{2,1,0:T(2,128)S(1)}, u32[]{:S(2)}, u32[]{:S(2)}) collective-permute-start(f32[18,2,1440]{2,1,0:T(2,128)} %get-tuple-element.122), channel_id=1, source_target_pairs={{1,0},{2,1},{3,2},{5,4},{6,5},{7,6},{9,8},{10,9},{11,10},{13,12},{... | collective-permute-start | bytes 622088 | tf_op jit(solution)/shard_map/while/body/eval_jaxpr/ppermute | solution.py:17
  74.4 7.9 %collective-permute-start.1 = (f32[18,2,1440]{2,1,0:T(2,128)S(1)}, f32[18,2,1440]{2,1,0:T(2,128)S(1)}, u32[]{:S(2)}, u32[]{:S(2)}) collective-permute-start(f32[18,2,1440]{2,1,0:T(2,128)S(1)} %get-tuple-element.123), channel_id=1, source_target_pairs={{0,1},{1,2},{2,3},{4,5},{5,6},{6,7},{8,9},{9,10},{10,11},{12,13},{... | collective-permute-start | bytes 622088 | tf_op jit(solution)/shard_map/while/body/eval_jaxpr/ppermute | solution.py:16
  96.9 79.6 %all-to-all-start = ((f32[18,8,4320]{2,0,1:T(8,128)}), f32[18,8,4320]{2,0,1:T(8,128)S(1)}, u32[]{:S(2)}, u32[]{:S(2)}) async-start(f32[18,8,4320]{2,0,1:T(8,128)} %copy.8), calls=%async_computation | async-start | bytes 6684672 | tf_op jit(solution)/shard_map/all_to_all | solution.py:54
  178.1 4.2 %copy-start.2 = (f32[144,144]{1,0:T(8,128)S(1)}, f32[144,144]{1,0:T(8,128)}, u32[]{:S(2)}) copy-start(f32[144,144]{1,0:T(8,128)} %param.10) | copy-start | bytes 248836
where the time goes:
time: 273 us; the launch traced here: 272 us
  blocking collectives  81.2 us (30%)
  waiting for transfers between devices  76.4 us (28%)
  starting transfers between devices  42.6 us (16%)
  local copies, waits for them, and re-layouts  37 us (14%)
  other arithmetic  26.6 us (10%)
  matrix products  8.1 us (3%)
    all_to_all x1, blocking collectives, local(): lax.all_to_all(mixed_cols, 'lev', split_axis=0, concat_axis=1, tiled=True)  81.2 us
    all_to_all x1, waiting for transfers between devices, local(): lax.all_to_all(flattened, 'lev', split_axis=1, concat_axis=0, tiled=True)  71.3 us
    ppermute x5, starting transfers between devices, padded_2(): before = lax.ppermute(last, axis, up)  30.4 us
    select_n x10, other arithmetic, sweep(): return jnp.where(inside, result, jnp.zeros((), jnp.float32))  23.7 us
    slice x15, local copies, waits for them, and re-layouts, sweep(): jnp.roll(middle_rows, -1, 2)  15.8 us
    all_to_all x3, local copies, waits for them, and re-layouts, local(): lax.all_to_all(flattened, 'lev', split_axis=1, concat_axis=0, tiled=True)  7.75 us
    ppermute x5, starting transfers between devices, padded_2(): after = lax.ppermute(leading, axis, down)  6.4 us
    all_to_all x1, starting transfers between devices, local(): lax.all_to_all(flattened, 'lev', split_axis=1, concat_axis=0, tiled=True)  5.81 us
  transfers between devices with their start and end apart: 11, of which 6 were waited for; matrix products, arithmetic and copies ran while one was open for 1% of the time, Pallas kernels for 0%

commit v1 on v0

--- a/solution.py
+++ b/solution.py
@@ -51,7 +51,10 @@
         ground_level.reshape(lat_rows * lon_cells), col_start, block_cols
     )
     total_levels = balance.shape[0]
-    columns = lax.all_to_all(flattened, "lev", split_axis=1, concat_axis=0, tiled=True)
+    columns = jnp.concatenate(
+        lax.all_to_all(jnp.stack(jnp.split(flattened, lax.axis_size("lev"), axis=1)), "lev", 0, 0),
+        axis=0,
+    )
     mixed_cols = jnp.dot(
         balance, columns, precision=lax.Precision.HIGHEST, preferred_element_type=jnp.float32
     )

time: 273 us -> 282 us (1.033)
  local copies, waits for them, and re-layouts: 37 us -> 45.8 us
    unnamed x8 -> x17, local copies, waits for them, and re-layouts: 1.8 us -> 12.3 us
    all_to_all x3 -> x0, local copies, waits for them, and re-layouts: 7.75 us -> none  [local(): lax.all_to_all(flattened, 'lev', split_axis=1, concat_axis=0, tiled=True)]
    reshape x0 -> x2, local copies, waits for them, and re-layouts: none -> 5.18 us  [the longest x1 3.56 us: local(): flattened = smoothed.reshape(levels_here, lat_rows * lon_cells)]
where the time goes in v1:
time: 282 us; the launch traced here: 281 us
  blocking collectives  81.2 us (29%)
  waiting for transfers between devices  76.4 us (27%)
  local copies, waits for them, and re-layouts  45.8 us (16%)
  starting transfers between devices  42.6 us (15%)
  other arithmetic  26.6 us (9%)
  matrix products  8.1 us (3%)
    all_to_all x1, blocking collectives, local(): lax.all_to_all(mixed_cols, 'lev', split_axis=0, concat_axis=1, tiled=True)  81.2 us
    all_to_all x1, waiting for transfers between devices, local(): lax.all_to_all(jnp.stack(jnp.split(flattened, lax.axis_size('lev'), axis=...  71.3 us
    ppermute x5, starting transfers between devices, padded_2(): before = lax.ppermute(last, axis, up)  30.4 us
    select_n x10, other arithmetic, sweep(): return jnp.where(inside, result, jnp.zeros((), jnp.float32))  23.7 us
    slice x15, local copies, waits for them, and re-layouts, sweep(): jnp.roll(middle_rows, -1, 2)  15.8 us
    unnamed x17, local copies, waits for them, and re-layouts  12.3 us
    ppermute x5, starting transfers between devices, padded_2(): after = lax.ppermute(leading, axis, down)  6.4 us
    all_to_all x1, starting transfers between devices, local(): lax.all_to_all(jnp.stack(jnp.split(flattened, lax.axis_size('lev'), axis=...  5.81 us
  transfers between devices with their start and end apart: 11, of which 6 were waited for; matrix products, arithmetic and copies ran while one was open for 1% of the time, Pallas kernels for 0%

profile of v1, /device:TPU:0, one launch (start us, length us, event | category | flops | bytes accessed | tf_op | source)
XLA Modules:
  0.0 281.2 jit_solution(15106866871369911760)
XLA Ops:
  1.8 89.0 %while.12 = (s32[]{:T(128)}, f32[18,24,1440]{2,1,0:T(8,128)S(1)}, s32[]{:T(128)}, s32[]{:T(128)}, f32[18,1,1]{0,2,1:T(1,128)S(1)}, /*index=5*/s32[]{:T(128)}) while((s32[]{:T(128)}, f32[18,24,1440]{2,1,0:T(8,128)S(1)}, s32[]{:T(128)}, s32[]{:T(128)}, f32[18,1,1]{0,2,1:T(1,128)S(1)}, /*index=5*/s32[]{:T(128)}) %tuple.41), condition=%wide.region_1.2_spmd, body=%wide.region_0.1_spmd.sunk | while | flops 18455240 | bytes 57635248 | solution.py:45
  3.9 3.0 %collective-permute-start.1 = (f32[18,2,1440]{2,1,0:T(2,128)S(1)}, f32[18,2,1440]{2,1,0:T(2,128)S(1)}, u32[]{:S(2)}, u32[]{:S(2)}) collective-permute-start(f32[18,2,1440]{2,1,0:T(2,128)S(1)} %get-tuple-element.123), channel_id=1, source_target_pairs={{0,1},{1,2},{2,3},{4,5},{5,6},{6,7},{8,9},{9,10},{10,11},{12,13},{... | collective-permute-start | bytes 622088 | tf_op jit(solution)/shard_map/while/body/eval_jaxpr/ppermute | solution.py:16
  8.6 1.8 fusion.39
  10.4 3.1 %fusion.40 = f32[18,26,1440]{2,1,0:T(8,128)S(1)} fusion(f32[18,2,1440]{2,1,0:T(2,128)S(1)} %collective-permute-done, f32[18,24,1440]{2,1,0:T(8,128)S(1)} %get-tuple-element.137, f32[18,2,1440]{2,1,0:T(2,128)S(1)} %collective-permute-done.1, f32[18,26,1439]{2,1,0:T(8,128)S(1)} %get-tuple-element.124, f32[18,26,1439]{2,1,0:T(8,128)S(1)} %get-tuple-element.125, ...), kind=kLoop, calls=%fused_computation.6.clone.1 | loop fusion | flops 10782720 | bytes 13682114 | tf_op jit(solution)/shard_map/while/body/eval_jaxpr/jit(_where)/select_n | solution.py:39
  18.7 6.9 %collective-permute-start.1 = (f32[18,2,1440]{2,1,0:T(2,128)S(1)}, f32[18,2,1440]{2,1,0:T(2,128)S(1)}, u32[]{:S(2)}, u32[]{:S(2)}) collective-permute-start(f32[18,2,1440]{2,1,0:T(2,128)S(1)} %get-tuple-element.123), channel_id=1, source_target_pairs={{0,1},{1,2},{2,3},{4,5},{5,6},{6,7},{8,9},{9,10},{10,11},{12,13},{... | collective-permute-start | bytes 622088 | tf_op jit(solution)/shard_map/while/body/eval_jaxpr/ppermute | solution.py:16
  29.1 3.1 %fusion.40 = f32[18,26,1440]{2,1,0:T(8,128)S(1)} fusion(f32[18,2,1440]{2,1,0:T(2,128)S(1)} %collective-permute-done, f32[18,24,1440]{2,1,0:T(8,128)S(1)} %get-tuple-element.137, f32[18,2,1440]{2,1,0:T(2,128)S(1)} %collective-permute-done.1, f32[18,26,1439]{2,1,0:T(8,128)S(1)} %get-tuple-element.124, f32[18,26,1439]{2,1,0:T(8,128)S(1)} %get-tuple-element.125, ...), kind=kLoop, calls=%fused_computation.6.clone.1 | loop fusion | flops 10782720 | bytes 13682114 | tf_op jit(solution)/shard_map/while/body/eval_jaxpr/jit(_where)/select_n | solution.py:39
  37.3 6.8 %collective-permute-start.1 = (f32[18,2,1440]{2,1,0:T(2,128)S(1)}, f32[18,2,1440]{2,1,0:T(2,128)S(1)}, u32[]{:S(2)}, u32[]{:S(2)}) collective-permute-start(f32[18,2,1440]{2,1,0:T(2,128)S(1)} %get-tuple-element.123), channel_id=1, source_target_pairs={{0,1},{1,2},{2,3},{4,5},{5,6},{6,7},{8,9},{9,10},{10,11},{12,13},{... | collective-permute-start | bytes 622088 | tf_op jit(solution)/shard_map/while/body/eval_jaxpr/ppermute | solution.py:16
  47.6 3.1 %fusion.40 = f32[18,26,1440]{2,1,0:T(8,128)S(1)} fusion(f32[18,2,1440]{2,1,0:T(2,128)S(1)} %collective-permute-done, f32[18,24,1440]{2,1,0:T(8,128)S(1)} %get-tuple-element.137, f32[18,2,1440]{2,1,0:T(2,128)S(1)} %collective-permute-done.1, f32[18,26,1439]{2,1,0:T(8,128)S(1)} %get-tuple-element.124, f32[18,26,1439]{2,1,0:T(8,128)S(1)} %get-tuple-element.125, ...), kind=kLoop, calls=%fused_computation.6.clone.1 | loop fusion | flops 10782720 | bytes 13682114 | tf_op jit(solution)/shard_map/while/body/eval_jaxpr/jit(_where)/select_n | solution.py:39
  55.9 6.8 %collective-permute-start.1 = (f32[18,2,1440]{2,1,0:T(2,128)S(1)}, f32[18,2,1440]{2,1,0:T(2,128)S(1)}, u32[]{:S(2)}, u32[]{:S(2)}) collective-permute-start(f32[18,2,1440]{2,1,0:T(2,128)S(1)} %get-tuple-element.123), channel_id=1, source_target_pairs={{0,1},{1,2},{2,3},{4,5},{5,6},{6,7},{8,9},{9,10},{10,11},{12,13},{... | collective-permute-start | bytes 622088 | tf_op jit(solution)/shard_map/while/body/eval_jaxpr/ppermute | solution.py:16
  66.1 3.1 %fusion.40 = f32[18,26,1440]{2,1,0:T(8,128)S(1)} fusion(f32[18,2,1440]{2,1,0:T(2,128)S(1)} %collective-permute-done, f32[18,24,1440]{2,1,0:T(8,128)S(1)} %get-tuple-element.137, f32[18,2,1440]{2,1,0:T(2,128)S(1)} %collective-permute-done.1, f32[18,26,1439]{2,1,0:T(8,128)S(1)} %get-tuple-element.124, f32[18,26,1439]{2,1,0:T(8,128)S(1)} %get-tuple-element.125, ...), kind=kLoop, calls=%fused_computation.6.clone.1 | loop fusion | flops 10782720 | bytes 13682114 | tf_op jit(solution)/shard_map/while/body/eval_jaxpr/jit(_where)/select_n | solution.py:39
  74.4 6.8 %collective-permute-start.1 = (f32[18,2,1440]{2,1,0:T(2,128)S(1)}, f32[18,2,1440]{2,1,0:T(2,128)S(1)}, u32[]{:S(2)}, u32[]{:S(2)}) collective-permute-start(f32[18,2,1440]{2,1,0:T(2,128)S(1)} %get-tuple-element.123), channel_id=1, source_target_pairs={{0,1},{1,2},{2,3},{4,5},{5,6},{6,7},{8,9},{9,10},{10,11},{12,13},{... | collective-permute-start | bytes 622088 | tf_op jit(solution)/shard_map/while/body/eval_jaxpr/ppermute | solution.py:16
  84.6 3.1 %fusion.40 = f32[18,26,1440]{2,1,0:T(8,128)S(1)} fusion(f32[18,2,1440]{2,1,0:T(2,128)S(1)} %collective-permute-done, f32[18,24,1440]{2,1,0:T(8,128)S(1)} %get-tuple-element.137, f32[18,2,1440]{2,1,0:T(2,128)S(1)} %collective-permute-done.1, f32[18,26,1439]{2,1,0:T(8,128)S(1)} %get-tuple-element.124, f32[18,26,1439]{2,1,0:T(8,128)S(1)} %get-tuple-element.125, ...), kind=kLoop, calls=%fused_computation.6.clone.1 | loop fusion | flops 10782720 | bytes 13682114 | tf_op jit(solution)/shard_map/while/body/eval_jaxpr/jit(_where)/select_n | solution.py:39
  90.8 3.6 %reshape.40 = f32[18,34560]{1,0:T(8,128)} reshape(f32[18,24,1440]{2,1,0:T(8,128)S(1)} %get-tuple-element.64) | data formatting | bytes 4976640 | tf_op jit(solution)/shard_map/reshape | solution.py:46
  94.3 1.9 fusion.22
  96.3 1.9 fusion.21
  98.2 1.9 fusion.20
  100.2 1.9 fusion.19
  105.7 5.8 %all-to-all-start = ((f32[8,18,4320]{2,1,0:T(8,128)}), f32[8,18,4320]{2,1,0:T(8,128)S(1)}, u32[]{:S(2)}, u32[]{:S(2)}) async-start(f32[8,18,4320]{2,1,0:T(8,128)} %fusion.15), calls=%async_computation | async-start | bytes 6684672 | tf_op jit(solution)/shard_map/all_to_all | solution.py:55
  114.1 71.3 %all-to-all-done = f32[8,18,4320]{2,1,0:T(8,128)S(1)} async-done(((f32[8,18,4320]{2,1,0:T(8,128)}), f32[8,18,4320]{2,1,0:T(8,128)S(1)}, u32[]{:S(2)}, u32[]{:S(2)}) %all-to-all-start) | async-done | bytes 2488352 | tf_op jit(solution)/shard_map/all_to_all | solution.py:55
  186.9 4.2 %fusion.27 = f32[4320,144]{0,1:T(8,128)S(1)} fusion(f32[144,4320]{1,0:T(8,128)} %reshape.41, f32[144,144]{1,0:T(8,128)S(1)} %copy-done), kind=kOutput, calls=%fused_computation.46 | convolution fusion | flops 1074954240 | bytes 5059584 | tf_op jit(solution)/shard_map/dot_general | solution.py:58
  191.1 3.9 %fusion.14 = f32[144,4320]{1,0:T(8,128)} fusion(f32[4320,144]{0,1:T(8,128)S(1)} %fusion.27, f32[144,144]{1,0:T(8,128)S(1)} %copy-done.3, s32[4320]{0:T(1024)S(1)} %dynamic_slice.3), kind=kOutput, calls=%fused_computation.24 | convolution fusion | flops 1076198400 | bytes 5076864 | tf_op jit(solution)/shard_map/dot_general | solution.py:61
  195.1 1.9 all_to_all.16
  196.9 81.2 %all_to_all.21 = f32[8,18,4320]{2,1,0:T(8,128)S(1)} all-to-all(f32[8,18,4320]{2,1,0:T(8,128)S(1)} %all_to_all.16), channel_id=1, replica_groups=mesh['lev'=8,'tile'=4] {'lev'}, dimensions={0} | all-to-all | bytes 4976640 | tf_op jit(solution)/shard_map/all_to_all | solution.py:66
  278.9 2.3 reshape.42
  (72 shorter events, 51.3 us)
Async XLA Ops:
  0.0 186.9 %copy-start = (f32[144,144]{1,0:T(8,128)S(1)}, f32[144,144]{1,0:T(8,128)}, u32[]{:S(2)}) copy-start(f32[144,144]{1,0:T(8,128)} %param.9) | copy-start | bytes 248836
  0.0 1.8 copy-start.1
  0.0 1.8 copy-start.4
  2.6 4.4 %collective-permute-start = (f32[18,2,1440]{2,1,0:T(2,128)}, f32[18,2,1440]{2,1,0:T(2,128)S(1)}, u32[]{:S(2)}, u32[]{:S(2)}) collective-permute-start(f32[18,2,1440]{2,1,0:T(2,128)} %get-tuple-element.122), channel_id=1, source_target_pairs={{1,0},{2,1},{3,2},{5,4},{6,5},{7,6},{9,8},{10,9},{11,10},{13,12},{... | collective-permute-start | bytes 622088 | tf_op jit(solution)/shard_map/while/body/eval_jaxpr/ppermute | solution.py:17
  3.9 4.1 %collective-permute-start.1 = (f32[18,2,1440]{2,1,0:T(2,128)S(1)}, f32[18,2,1440]{2,1,0:T(2,128)S(1)}, u32[]{:S(2)}, u32[]{:S(2)}) collective-permute-start(f32[18,2,1440]{2,1,0:T(2,128)S(1)} %get-tuple-element.123), channel_id=1, source_target_pairs={{0,1},{1,2},{2,3},{4,5},{5,6},{6,7},{8,9},{9,10},{10,11},{12,13},{... | collective-permute-start | bytes 622088 | tf_op jit(solution)/shard_map/while/body/eval_jaxpr/ppermute | solution.py:16
  17.4 8.3 %collective-permute-start = (f32[18,2,1440]{2,1,0:T(2,128)}, f32[18,2,1440]{2,1,0:T(2,128)S(1)}, u32[]{:S(2)}, u32[]{:S(2)}) collective-permute-start(f32[18,2,1440]{2,1,0:T(2,128)} %get-tuple-element.122), channel_id=1, source_target_pairs={{1,0},{2,1},{3,2},{5,4},{6,5},{7,6},{9,8},{10,9},{11,10},{13,12},{... | collective-permute-start | bytes 622088 | tf_op jit(solution)/shard_map/while/body/eval_jaxpr/ppermute | solution.py:17
  18.7 8.0 %collective-permute-start.1 = (f32[18,2,1440]{2,1,0:T(2,128)S(1)}, f32[18,2,1440]{2,1,0:T(2,128)S(1)}, u32[]{:S(2)}, u32[]{:S(2)}) collective-permute-start(f32[18,2,1440]{2,1,0:T(2,128)S(1)} %get-tuple-element.123), channel_id=1, source_target_pairs={{0,1},{1,2},{2,3},{4,5},{5,6},{6,7},{8,9},{9,10},{10,11},{12,13},{... | collective-permute-start | bytes 622088 | tf_op jit(solution)/shard_map/while/body/eval_jaxpr/ppermute | solution.py:16
  36.1 8.1 %collective-permute-start = (f32[18,2,1440]{2,1,0:T(2,128)}, f32[18,2,1440]{2,1,0:T(2,128)S(1)}, u32[]{:S(2)}, u32[]{:S(2)}) collective-permute-start(f32[18,2,1440]{2,1,0:T(2,128)} %get-tuple-element.122), channel_id=1, source_target_pairs={{1,0},{2,1},{3,2},{5,4},{6,5},{7,6},{9,8},{10,9},{11,10},{13,12},{... | collective-permute-start | bytes 622088 | tf_op jit(solution)/shard_map/while/body/eval_jaxpr/ppermute | solution.py:17
  37.3 7.9 %collective-permute-start.1 = (f32[18,2,1440]{2,1,0:T(2,128)S(1)}, f32[18,2,1440]{2,1,0:T(2,128)S(1)}, u32[]{:S(2)}, u32[]{:S(2)}) collective-permute-start(f32[18,2,1440]{2,1,0:T(2,128)S(1)} %get-tuple-element.123), channel_id=1, source_target_pairs={{0,1},{1,2},{2,3},{4,5},{5,6},{6,7},{8,9},{9,10},{10,11},{12,13},{... | collective-permute-start | bytes 622088 | tf_op jit(solution)/shard_map/while/body/eval_jaxpr/ppermute | solution.py:16
  54.6 8.1 %collective-permute-start = (f32[18,2,1440]{2,1,0:T(2,128)}, f32[18,2,1440]{2,1,0:T(2,128)S(1)}, u32[]{:S(2)}, u32[]{:S(2)}) collective-permute-start(f32[18,2,1440]{2,1,0:T(2,128)} %get-tuple-element.122), channel_id=1, source_target_pairs={{1,0},{2,1},{3,2},{5,4},{6,5},{7,6},{9,8},{10,9},{11,10},{13,12},{... | collective-permute-start | bytes 622088 | tf_op jit(solution)/shard_map/while/body/eval_jaxpr/ppermute | solution.py:17
  55.9 7.9 %collective-permute-start.1 = (f32[18,2,1440]{2,1,0:T(2,128)S(1)}, f32[18,2,1440]{2,1,0:T(2,128)S(1)}, u32[]{:S(2)}, u32[]{:S(2)}) collective-permute-start(f32[18,2,1440]{2,1,0:T(2,128)S(1)} %get-tuple-element.123), channel_id=1, source_target_pairs={{0,1},{1,2},{2,3},{4,5},{5,6},{6,7},{8,9},{9,10},{10,11},{12,13},{... | collective-permute-start | bytes 622088 | tf_op jit(solution)/shard_map/while/body/eval_jaxpr/ppermute | solution.py:16
  73.1 8.1 %collective-permute-start = (f32[18,2,1440]{2,1,0:T(2,128)}, f32[18,2,1440]{2,1,0:T(2,128)S(1)}, u32[]{:S(2)}, u32[]{:S(2)}) collective-permute-start(f32[18,2,1440]{2,1,0:T(2,128)} %get-tuple-element.122), channel_id=1, source_target_pairs={{1,0},{2,1},{3,2},{5,4},{6,5},{7,6},{9,8},{10,9},{11,10},{13,12},{... | collective-permute-start | bytes 622088 | tf_op jit(solution)/shard_map/while/body/eval_jaxpr/ppermute | solution.py:17
  74.4 7.9 %collective-permute-start.1 = (f32[18,2,1440]{2,1,0:T(2,128)S(1)}, f32[18,2,1440]{2,1,0:T(2,128)S(1)}, u32[]{:S(2)}, u32[]{:S(2)}) collective-permute-start(f32[18,2,1440]{2,1,0:T(2,128)S(1)} %get-tuple-element.123), channel_id=1, source_target_pairs={{0,1},{1,2},{2,3},{4,5},{5,6},{6,7},{8,9},{9,10},{10,11},{12,13},{... | collective-permute-start | bytes 622088 | tf_op jit(solution)/shard_map/while/body/eval_jaxpr/ppermute | solution.py:16
  94.3 7.8 %copy-start.2 = (f32[18,34560]{1,0:T(8,128)S(1)}, f32[18,34560]{1,0:T(8,128)}, u32[]{:S(2)}) copy-start(f32[18,34560]{1,0:T(8,128)} %reshape.40) | copy-start | bytes 7464964
  105.7 79.6 %all-to-all-start = ((f32[8,18,4320]{2,1,0:T(8,128)}), f32[8,18,4320]{2,1,0:T(8,128)S(1)}, u32[]{:S(2)}, u32[]{:S(2)}) async-start(f32[8,18,4320]{2,1,0:T(8,128)} %fusion.15), calls=%async_computation | async-start | bytes 6684672 | tf_op jit(solution)/shard_map/all_to_all | solution.py:55
  186.9 4.2 %copy-start.3 = (f32[144,144]{1,0:T(8,128)S(1)}, f32[144,144]{1,0:T(8,128)}, u32[]{:S(2)}) copy-start(f32[144,144]{1,0:T(8,128)} %param.10) | copy-start | bytes 248836
